TPU v7x, 512 devices: a whole 4x8x8 slice. The times are simulated.
512 devices in a mesh: group: 8 (over z), dom: 64 (over y, x, core).
Axes of the slice: x: 4, y: 8, z: 8, core: 2. Of those that a mesh axis runs over, the one named last changes fastest.
Arguments:
- orbitals: bfloat16 [1572864, 512], P(('group', 'dom')), may hold values from -6 to 6
- density_rows: bfloat16 [16384, 2048], P(('group', 'dom')), may hold values from -0.01171875 to 0.01171875
- near_blocks: int32 [512, 32], P(('group', 'dom')), may hold values from 0 to 127, as said below
- leaf_coords: int32 [3, 3072], P(None, ('group', 'dom')), may hold values from 0 to 127, as said below
- near_leaves: int32 [3072, 3], P(('group', 'dom')), may hold values from 0 to 17, as said below
- leaf_basis: float32 [64, 1572864], P(None, ('group', 'dom')), may hold values from -2 to 2
- leaf_transfer: float32 [3072, 64, 64], P(('group', 'dom')), may hold values from -0.75 to 0.75
- dev_transfer: float32 [512, 64, 64], P(('group', 'dom')), may hold values from -0.375 to 0.375
- dev_far: int32 [512, 64], P(('group', 'dom')), may hold values 0 or 1
- group_far: int32 [8, 8], P('group'), may hold values 0 or 1
Outputs:
- density: float32 [1572864], P(('group', 'dom'))
- hartree: float32 [1572864], P(('group', 'dom'))
Inputs may be any that keep to these rules, and one draw needn't show every extreme that they name: `near_blocks`: each row names 32 distinct blocks of its own coarse domain; block b is rows b * 16 to b * 16 + 15 of the domain's density matrix, held by the device of dom index b // 2. The first 2 entries of every row of a domain are the same: all blocks of one device of that domain, in order. Every other entry is a block held by a device whose dom index differs from the row's own by at most 8, counted cyclically over the 64 dom indices. `near_leaves`: each row names 3 distinct window positions, among them the leaf's own position 6 + (t mod 6) for row t. `leaf_coords`: distinct positions for all leaves.
All inputs are finite; a program needn't handle non-finite values. No bound on the sum of `dev_far` or of `group_far` on one device may be relied on, other than what follows from the above.
Results may differ from a plain program's by a relative error of at most 0.0003.
Values may be sent and summed in bfloat16 or wider, within the bound.
A program may use at most 128 MiB of HBM per device.

v0:
```python
import math
import jax
import jax.numpy as jnp
from jax import lax
from jax.sharding import PartitionSpec as P

SIDE = 8
LEAF = 512
CHEB = 4
BW = 16
NEARL = 3
vol_weight = 0.1
soft_square = 1.0


def with_halo(value, sides, width):
    for axis, dim in sides:
        peers, length = (lax.axis_size(axis), value.shape[dim])
        up = [(i, (i + 1) % peers) for i in range(peers - 1)]
        down = [(j, i) for i, j in up]
        last = lax.slice_in_dim(value, length - width, length, axis=dim)
        first = lax.slice_in_dim(value, 0, width, axis=dim)
        before = lax.ppermute(last, axis, up)
        after = lax.ppermute(first, axis, down)
        value = jnp.concatenate([before, value, after], axis=dim)
    return value


def coulomb(target, source):
    diff_x = target[0][:, None] - source[0][None, :]
    diff_y = target[1][:, None] - source[1][None, :]
    diff_z = target[2][:, None] - source[2][None, :]
    return 1.0 / jnp.sqrt(diff_x * diff_x + diff_y * diff_y + diff_z * diff_z + soft_square)


def cluster_nodes(bounds):
    steps_idx = jnp.arange(CHEB).astype(jnp.float32)
    cheb_points = jnp.cos((2.0 * steps_idx + 1.0) * (math.pi / (2.0 * CHEB)))
    centre = 0.5 * (bounds[:3] + bounds[3:])
    half_size = 0.5 * (bounds[3:] - bounds[:3])
    along = centre[:, None] + half_size[:, None] * cheb_points[None, :]
    node_index = jnp.arange(CHEB * CHEB * CHEB)
    first = node_index // (CHEB * CHEB)
    second = node_index // CHEB % CHEB
    third = node_index % CHEB
    return jnp.stack([along[0][first], along[1][second], along[2][third]])


def point_offsets():
    place = jnp.arange(LEAF)
    return jnp.stack([place // (SIDE * SIDE), place // SIDE % SIDE, place % SIDE]).astype(
        jnp.float32
    )


def far_coupling(own_nodes, other_bounds, mask_row, moments):
    other_nodes = jax.vmap(cluster_nodes)(other_bounds)
    coupling = jax.vmap(lambda other: coulomb(own_nodes, other))(other_nodes)
    coupling = coupling * mask_row.astype(jnp.float32)[:, None, None]
    return vol_weight * jnp.einsum("srq,sq->r", coupling, moments, precision=lax.Precision.HIGHEST)


def local(
    orbitals,
    density_rows,
    near_blocks,
    leaf_coords,
    near_leaves,
    leaf_basis,
    leaf_transfer,
    dev_transfer,
    dev_far,
    group_far,
):
    near_list = near_blocks[0]
    near_width = orbitals.shape[1]
    blocks_group = density_rows.shape[1] // BW
    rows_global = (near_list[:, None] * BW + jnp.arange(BW)[None, :]).reshape(-1)
    row_piece = lax.all_gather(density_rows, "dom", axis=0, tiled=True)
    piece_rows = row_piece.shape[0]
    columns = jnp.take(row_piece.reshape(piece_rows, blocks_group, BW), near_list, axis=1).reshape(
        piece_rows, near_width
    )
    inside = (rows_global >= 0) & (rows_global < piece_rows)
    chosen = jnp.take(columns, jnp.clip(rows_global, 0, piece_rows - 1), axis=0)
    local_matrix = jnp.where(
        inside[:, None], chosen, jnp.zeros((near_width, near_width), jnp.bfloat16)
    )
    product = jnp.dot(orbitals, local_matrix, preferred_element_type=jnp.float32)
    density = jnp.sum(product * orbitals.astype(jnp.float32), axis=1)
    leaf_count = leaf_coords.shape[1]
    coords_f = leaf_coords.astype(jnp.float32)
    points = SIDE * coords_f.T[:, :, None] + point_offsets()[None]
    rho_leaf = density.reshape(leaf_count, LEAF)
    packed = jnp.concatenate([points, rho_leaf[:, None, :]], axis=1)
    window = with_halo(packed, (("dom", 0),), leaf_count)

    def near_one(leaf_index):
        own_points = points[leaf_index]
        running = jnp.zeros((LEAF,), jnp.float32)
        for near_slot in range(NEARL):
            source_leaf = window[near_leaves[leaf_index, near_slot]]
            running = running + jnp.dot(
                coulomb(own_points, source_leaf[:3]),
                source_leaf[3],
                precision=lax.Precision.HIGHEST,
            )
        return running

    near_part = lax.map(near_one, jnp.arange(leaf_count)) * vol_weight
    rank = leaf_basis.shape[0]
    leaf_bases = leaf_basis.reshape(rank, leaf_count, LEAF)
    leaf_mom = jnp.einsum("rlp,lp->lr", leaf_bases, rho_leaf, precision=lax.Precision.HIGHEST)
    dev_mom = jnp.einsum("lqr,lq->r", leaf_transfer, leaf_mom, precision=lax.Precision.HIGHEST)
    bounds = jnp.concatenate(
        [SIDE * jnp.min(coords_f, axis=1), SIDE * jnp.max(coords_f, axis=1) + (SIDE - 1)]
    )
    upward = jnp.einsum("qr,q->r", dev_transfer[0], dev_mom, precision=lax.Precision.HIGHEST)
    all_mom, all_bounds = (
        lax.all_gather(dev_mom[None], "dom", axis=0, tiled=True),
        lax.all_gather(bounds[None], "dom", axis=0, tiled=True),
    )
    group_mom = lax.psum(upward, "dom")
    dev_local = far_coupling(cluster_nodes(bounds), all_bounds, dev_far[0], all_mom)
    group_bounds = jnp.concatenate(
        [jnp.min(all_bounds[:, :3], axis=0), jnp.max(all_bounds[:, 3:], axis=0)]
    )
    coarse_mom, coarse_bounds = (
        lax.all_gather(group_mom[None], "group", axis=0, tiled=True),
        lax.all_gather(group_bounds[None], "group", axis=0, tiled=True),
    )
    group_local = far_coupling(cluster_nodes(group_bounds), coarse_bounds, group_far[0], coarse_mom)
    dev_total = dev_local + jnp.einsum(
        "qr,r->q", dev_transfer[0], group_local, precision=lax.Precision.HIGHEST
    )
    leaf_local = jnp.einsum("lqr,r->lq", leaf_transfer, dev_total, precision=lax.Precision.HIGHEST)
    far_part = jnp.einsum("rlp,lr->lp", leaf_bases, leaf_local, precision=lax.Precision.HIGHEST)
    hartree = (near_part + far_part).reshape(-1)
    return (density, hartree)


def solution(mesh):
    in_specs = (
        P(("group", "dom"), None),
        P(("group", "dom"), None),
        P(("group", "dom"), None),
        P(None, ("group", "dom")),
        P(("group", "dom"), None),
        P(None, ("group", "dom")),
        P(("group", "dom"), None, None),
        P(("group", "dom"), None, None),
        P(("group", "dom"), None),
        P("group", None),
    )
    out_specs = (P(("group", "dom")), P(("group", "dom")))
    return jax.shard_map(local, mesh=mesh, in_specs=in_specs, out_specs=out_specs, check_vma=False)
```

profile of v0, /device:TPU:32, one launch (start us, length us, event | category | flops | bytes accessed | tf_op | source)
XLA Modules:
  0.0 532.1 jit_solution(10032816839666519139)
XLA Ops:
  7.2 0.7 all-gather.6.cloned.1.call-update
  7.9 0.7 bitcast_multiply_fusion.1
  8.8 1.3 dynamic-slice.2
  10.1 1.3 dynamic-slice
  13.3 0.7 compare_and_fusion
  14.1 0.8 convert_reduce_fusion.1
  15.3 4.7 copy.52
  20.5 80.6 %all-gather.6.cloned.1.call-done = bf16[2048,2048]{1,0:T(8,128)(2,1)} async-done(((bf16[32,2048]{1,0:T(8,128)(2,1)}), bf16[2048,2048]{1,0:T(8,128)(2,1)}) %all-gather.6.cloned.1.call-update) | async-done | bytes 8388624 | tf_op jit(solution)/shard_map/all_gather | solution.py:79
  101.1 12.3 %copy.50 = bf16[2048,2048]{0,1:T(8,128)(2,1)} copy(bf16[2048,2048]{1,0:T(8,128)(2,1)} %all-gather.6.cloned.1.call-done) | data formatting | bytes 16777216 | tf_op jit(solution)/shard_map/all_gather | solution.py:79
  113.3 4.1 gather_fusion
  117.4 2.5 copy.51
  119.9 1.8 broadcast_select_fusion
  121.7 2.0 gather_fusion.1
  123.7 5.0 fusion.63
  128.8 5.3 %collective-permute-start.1 = (f32[6,4,512]{2,1,0:T(4,128)S(1)}, f32[6,4,512]{2,1,0:T(4,128)S(1)}, u32[]{:S(2)}, u32[]{:S(2)}) collective-permute-start(f32[6,4,512]{2,1,0:T(4,128)S(1)} %pad_maximum_fusion.1), channel_id=1, source_target_pairs={{1,0},{2,1},{3,2},{4,3},{5,4},{6,5},{7,6},{8,7},{9,8},{10,9},{11,1... | collective-permute-start | bytes 147464 | tf_op jit(solution)/shard_map/ppermute | solution.py:24
  134.1 1.9 collective-permute-start
  136.0 0.7 fusion.96
  137.3 251.2 %all-reduce.3 = (f32[4096]{0:T(1024)S(1)}, f32[384]{0:T(512)S(1)}, f32[1,64]{1,0:T(1,128)S(1)}) all-reduce(f32[4096]{0:T(1024)S(1)} %bitcast_dynamic-update-slice_fusion, f32[384]{0:T(512)S(1)} %maximum_dynamic-update-slice_fusion, f32[1,64]{1,0:T(1,128)S(1)} %fusion.126), channel_id=3, replica_groups=mesh['group'=8,'dom'=64] {'dom'}, use_global_device_ids=true, to_apply=%add.1 | all-reduce | flops 4544 | bytes 36352
  388.6 17.1 %all-gather.3 = f32[8,1,64]{2,1,0:T(1,128)S(1)} all-gather(f32[1,1,64]{2,1,0:T(1,128)S(1)} %bitcast.298), channel_id=1, replica_groups=mesh['group'=8,'dom'=64] {'group'}, dimensions={0}, use_global_device_ids=true | all-gather | bytes 2304 | tf_op jit(solution)/shard_map/all_gather | solution.py:129
  406.2 14.9 %all-reduce.2 = f32[48]{0:T(128)S(1)} all-reduce(f32[48]{0:T(128)S(1)} %maximum_dynamic-update-slice_fusion.1), channel_id=4, replica_groups=mesh['group'=8,'dom'=64] {'group'}, use_global_device_ids=true, to_apply=%add.2 | all-reduce | flops 48 | bytes 384
  421.8 0.7 fusion.147
  422.5 0.7 fusion.148
  427.3 2.6 compare_select_fusion.23
  429.9 2.5 compare_select_fusion.24
  432.4 5.0 compare_select_fusion.11
  437.4 5.0 compare_select_fusion.12
  442.9 2.6 fusion.83
  446.8 77.9 %while.10 = (s32[]{:T(128)}, f32[6,512]{1,0:T(8,128)S(1)}, s32[6]{0:T(128)S(1)}, f32[6,3,512]{2,1,0:T(4,128)S(1)}, s32[6,3]{0,1:T(4,128)S(1)}, /*index=5*/f32[18...) while((s32[]{:T(128)}, f32[6,512]{1,0:T(8,128)S(1)}, ...), condition=%wide.region_2.3_spmd, body=%wide.region_1.2_spmd.sunk | while | flops 16516113 | bytes 110989 | solution.py:110
  455.5 1.4 fusion.172
  456.9 1.4 fusion.174
  458.3 1.4 fusion.173
  468.5 1.4 fusion.172
  469.9 1.4 fusion.174
  471.3 1.4 fusion.173
  481.5 1.4 fusion.172
  482.8 1.4 fusion.174
  484.2 1.4 fusion.173
  494.4 1.4 fusion.172
  495.8 1.4 fusion.174
  497.2 1.4 fusion.173
  501.2 0.6 constant_dynamic-slice_fusion.20
  507.4 1.4 fusion.172
  508.8 1.4 fusion.174
  510.2 1.4 fusion.173
  514.2 0.6 constant_dynamic-slice_fusion.20
  520.4 1.4 fusion.172
  521.8 1.4 fusion.174
  523.2 1.4 fusion.173
  (126 shorter events, 15.9 us)
Async XLA Ops:
  7.2 129.6 %copy-start = (f32[6,64,64]{2,1,0:T(8,128)S(1)}, f32[6,64,64]{2,1,0:T(8,128)}, u32[]{:S(2)}) copy-start(f32[6,64,64]{2,1,0:T(8,128)} %param.18) | copy-start | bytes 294916
  7.2 93.9 %all-gather.6.cloned.1.call-start = ((), (), s32[]{:S(2)}) async-start(), calls=%async_computation | async-start | bytes 8519680 | tf_op jit(solution)/shard_map/all_gather | solution.py:79
  15.2 5.1 copy-start.5
  15.2 5.1 copy-start.6
  15.2 5.1 copy-start.7
  123.7 12.3 %copy-start.1 = (f32[64,3072]{1,0:T(8,128)S(1)}, f32[64,3072]{1,0:T(8,128)}, u32[]{:S(2)}) copy-start(f32[64,3072]{1,0:T(8,128)} %param.17) | copy-start | bytes 2359300
  123.7 13.3 %copy-start.2 = (f32[1,64,64]{2,1,0:T(8,128)S(1)}, f32[1,64,64]{2,1,0:T(8,128)}, u32[]{:S(2)}) copy-start(f32[1,64,64]{2,1,0:T(8,128)} %param.19) | copy-start | bytes 49156
  128.7 318.0 %copy-start.3 = (f32[3072]{0:T(1024)}, f32[3072]{0:T(1024)S(1)}, u32[]{:S(2)}) copy-start(f32[3072]{0:T(1024)S(1)} %fusion.63) | copy-start | bytes 36868
  128.8 317.9 %collective-permute-start.1 = (f32[6,4,512]{2,1,0:T(4,128)S(1)}, f32[6,4,512]{2,1,0:T(4,128)S(1)}, u32[]{:S(2)}, u32[]{:S(2)}) collective-permute-start(f32[6,4,512]{2,1,0:T(4,128)S(1)} %pad_maximum_fusion.1), channel_id=1, source_target_pairs={{1,0},{2,1},{3,2},{4,3},{5,4},{6,5},{7,6},{8,7},{9,8},{10,9},{11,1... | collective-permute-start | bytes 147464 | tf_op jit(solution)/shard_map/ppermute | solution.py:24
  134.1 312.6 %collective-permute-start = (f32[6,4,512]{2,1,0:T(4,128)S(1)}, f32[6,4,512]{2,1,0:T(4,128)S(1)}, u32[]{:S(2)}, u32[]{:S(2)}) collective-permute-start(f32[6,4,512]{2,1,0:T(4,128)S(1)} %pad_maximum_fusion.1), channel_id=1, source_target_pairs={{0,1},{1,2},{2,3},{3,4},{4,5},{5,6},{6,7},{7,8},{8,9},{9,10},{10,1... | collective-permute-start | bytes 147464 | tf_op jit(solution)/shard_map/ppermute | solution.py:23
  442.9 3.9 copy-start.4
Sparse Core Ops, SparseCore 0:
  11.4 89.6 all-gather.5
where the time goes:
time: 534 us; the launch traced here: 532 us
  blocking collectives  283 us (53%)
  waiting for transfers between devices  81.2 us (15%)
  loops' own time  45.1 us (8%)
  local copies, waits for them, and re-layouts  43.1 us (8%)
  matrix products  35.3 us (7%)
  other arithmetic  20.4 us (4%)
  between operations  16.4 us (3%)
  starting transfers between devices  7.29 us (1%)
    unnamed x2, blocking collectives  266 us
    all_gather x1, waiting for transfers between devices, local(): row_piece = lax.all_gather(density_rows, 'dom', axis=0, tiled=True)  80.6 us
    another operation x1, loops' own time, local(): near_part = lax.map(near_one, jnp.arange(leaf_count)) * vol_weight  45.1 us
    dot_general x18, matrix products, near_one(): jnp.dot(coulomb(own_points, source_leaf[:3]), source_leaf[3], precision=l...  25 us
    all_gather x1, blocking collectives, local(): lax.all_gather(group_mom[None], 'group', axis=0, tiled=True)  17.1 us
    gather x7, other arithmetic, cluster_nodes(): return jnp.stack([along[0][first], along[1][second], along[2][third]])  15.1 us
    all_gather x1, local copies, waits for them, and re-layouts, local(): row_piece = lax.all_gather(density_rows, 'dom', axis=0, tiled=True)  12.3 us
  transfers between devices with their start and end apart: 3, of which 1 were waited for; matrix products, arithmetic and copies ran while one was open for 7% of the time, Pallas kernels for 0%

commit v1 on v0

--- a/solution.py
+++ b/solution.py
@@ -76,7 +76,9 @@
     near_width = orbitals.shape[1]
     blocks_group = density_rows.shape[1] // BW
     rows_global = (near_list[:, None] * BW + jnp.arange(BW)[None, :]).reshape(-1)
-    row_piece = lax.all_gather(density_rows, "dom", axis=0, tiled=True)
+    row_piece = jnp.concatenate(
+        lax.all_to_all(jnp.stack([density_rows] * lax.axis_size("dom")), "dom", 0, 0), axis=0
+    )
     piece_rows = row_piece.shape[0]
     columns = jnp.take(row_piece.reshape(piece_rows, blocks_group, BW), near_list, axis=1).reshape(
         piece_rows, near_width

time: 534 us -> 702 us (1.31)
  waiting for transfers between devices: 81.2 us -> 173 us
  local copies, waits for them, and re-layouts: 43.1 us -> 122 us
  between operations: 16.4 us -> 3.03 us
  starting transfers between devices: 7.29 us -> 19.9 us
    all_to_all x0 -> x1, waiting for transfers between devices: none -> 173 us  [local(): lax.all_to_all(jnp.stack([density_rows] * lax.axis_size('dom')), 'dom', 0...]
    all_gather x1 -> x0, waiting for transfers between devices: 80.6 us -> none  [local(): row_piece = lax.all_gather(density_rows, 'dom', axis=0, tiled=True)]
    another operation x0 -> x2, local copies, waits for them, and re-layouts: none -> 48.8 us  [the longest x1 43.6 us: local(): row_piece.reshape(piece_rows, blocks_group, BW)]
    all_to_all x0 -> x1, local copies, waits for them, and re-layouts: none -> 44.2 us  [local(): lax.all_to_all(jnp.stack([density_rows] * lax.axis_size('dom')), 'dom', 0...]
    all_gather x1 -> x0, local copies, waits for them, and re-layouts: 12.3 us -> none  [local(): row_piece = lax.all_gather(density_rows, 'dom', axis=0, tiled=True)]
    all_to_all x0 -> x1, starting transfers between devices: none -> 11.1 us  [local(): lax.all_to_all(jnp.stack([density_rows] * lax.axis_size('dom')), 'dom', 0...]
  transfers between devices with their start and end apart: 3 -> 3, of which waited for: 1 -> 1; matrix products, arithmetic and copies ran while one was open for 7% -> 5% of each run, Pallas kernels for 0% -> 0%
where the time goes in v1:
time: 702 us; the launch traced here: 700 us
  blocking collectives  283 us (40%)
  waiting for transfers between devices  173 us (25%)
  local copies, waits for them, and re-layouts  122 us (17%)
  loops' own time  45 us (6%)
  matrix products  35.3 us (5%)
  starting transfers between devices  19.9 us (3%)
  other arithmetic  18.3 us (3%)
    unnamed x2, blocking collectives  270 us
    all_to_all x1, waiting for transfers between devices, local(): lax.all_to_all(jnp.stack([density_rows] * lax.axis_size('dom')), 'dom', 0...  173 us
    another operation x1, loops' own time, local(): near_part = lax.map(near_one, jnp.arange(leaf_count)) * vol_weight  45 us
    all_to_all x1, local copies, waits for them, and re-layouts, local(): lax.all_to_all(jnp.stack([density_rows] * lax.axis_size('dom')), 'dom', 0...  44.2 us
    another operation x1, local copies, waits for them, and re-layouts, local(): row_piece.reshape(piece_rows, blocks_group, BW)  43.6 us
    dot_general x18, matrix products, near_one(): jnp.dot(coulomb(own_points, source_leaf[:3]), source_leaf[3], precision=l...  25 us
    gather x7, other arithmetic, cluster_nodes(): return jnp.stack([along[0][first], along[1][second], along[2][third]])  15.1 us
  transfers between devices with their start and end apart: 3, of which 1 were waited for; matrix products, arithmetic and copies ran while one was open for 5% of the time, Pallas kernels for 0%

profile of v1, /device:TPU:32, one launch (start us, length us, event | category | flops | bytes accessed | tf_op | source)
XLA Modules:
  0.0 700.1 jit_solution(8062636788484208269)
XLA Ops:
  0.6 5.2 stack.20
  5.9 11.1 %all-to-all-start = ((bf16[64,32,2048]{2,1,0:T(8,128)(2,1)}), bf16[64,32,2048]{2,1,0:T(8,128)(2,1)}, u32[]{:S(2)}, u32[]{:S(2)}) async-start(bf16[64,32,2048]{2,1,0:T(8,128)(2,1)} %stack.20), calls=%async_computation | async-start | bytes 16777216 | tf_op jit(solution)/shard_map/all_to_all | solution.py:80
  17.6 3.0 copy.52
  20.7 1.3 dynamic-slice
  23.2 1.3 dynamic-slice.2
  26.0 173.2 %all-to-all-done = bf16[64,32,2048]{2,1,0:T(8,128)(2,1)} async-done(((bf16[64,32,2048]{2,1,0:T(8,128)(2,1)}), bf16[64,32,2048]{2,1,0:T(8,128)(2,1)}, u32[]{:S(2)}, u32[]{:S(2)}) %all-to-all-start) | async-done | bytes 8388640 | tf_op jit(solution)/shard_map/all_to_all | solution.py:80
  199.2 44.2 %copy.50 = bf16[64,32,2048]{1,0,2:T(8,128)(2,1)} copy(bf16[64,32,2048]{2,1,0:T(8,128)(2,1)} %all-to-all-done) | data formatting | bytes 16777216 | tf_op jit(solution)/shard_map/all_to_all | solution.py:80
  243.4 43.6 %reshape_reshape.3 = bf16[2048,128,16]{0,2,1:T(8,128)(2,1)} reshape(bf16[64,32,2048]{1,0,2:T(8,128)(2,1)} %copy.50) | data formatting | bytes 16777216 | tf_op jit(solution)/shard_map/reshape;reshape | solution.py:83
  287.0 4.1 gather_fusion
  291.1 2.5 copy.51
  293.6 1.8 broadcast_select_fusion
  295.4 2.0 gather_fusion.1
  297.4 5.0 fusion.63
  302.4 1.9 collective-permute-start
  304.3 7.0 collective-permute-start.1
  311.3 0.7 fusion.96
  312.6 246.2 %all-reduce.3 = (f32[4096]{0:T(1024)S(1)}, f32[384]{0:T(512)S(1)}, f32[1,64]{1,0:T(1,128)S(1)}) all-reduce(f32[4096]{0:T(1024)S(1)} %bitcast_dynamic-update-slice_fusion, f32[384]{0:T(512)S(1)} %maximum_dynamic-update-slice_fusion, f32[1,64]{1,0:T(1,128)S(1)} %fusion.126), channel_id=3, replica_groups=mesh['group'=8,'dom'=64] {'dom'}, use_global_device_ids=true, to_apply=%add.1 | all-reduce | flops 4544 | bytes 36352
  559.1 0.7 fusion.147
  560.0 23.4 %all-reduce.2 = f32[48]{0:T(128)S(1)} all-reduce(f32[48]{0:T(128)S(1)} %maximum_dynamic-update-slice_fusion.1), channel_id=4, replica_groups=mesh['group'=8,'dom'=64] {'group'}, use_global_device_ids=true, to_apply=%add.2 | all-reduce | flops 48 | bytes 384
  585.8 13.4 %all-gather.3 = f32[8,1,64]{2,1,0:T(1,128)S(1)} all-gather(f32[1,1,64]{2,1,0:T(1,128)S(1)} %bitcast.298), channel_id=1, replica_groups=mesh['group'=8,'dom'=64] {'group'}, dimensions={0}, use_global_device_ids=true | all-gather | bytes 2304 | tf_op jit(solution)/shard_map/all_gather | solution.py:131
  599.2 0.7 fusion.148
  602.3 2.5 compare_select_fusion.23
  604.8 2.5 compare_select_fusion.24
  607.2 4.9 compare_select_fusion.11
  612.6 5.2 compare_select_fusion.12
  617.8 2.5 fusion.83
  621.7 77.8 %while.10 = (s32[]{:T(128)}, f32[6,512]{1,0:T(8,128)S(1)}, s32[6]{0:T(128)S(1)}, f32[6,3,512]{2,1,0:T(4,128)S(1)}, s32[6,3]{0,1:T(4,128)S(1)}, /*index=5*/f32[18...) while((s32[]{:T(128)}, f32[6,512]{1,0:T(8,128)S(1)}, ...), condition=%wide.region_2.3_spmd, body=%wide.region_1.2_spmd.sunk | while | flops 16516113 | bytes 110981 | solution.py:112
  630.4 1.4 fusion.174
  631.8 1.4 fusion.173
  633.2 1.4 fusion.172
  637.2 0.6 constant_dynamic-slice_fusion.20
  643.4 1.4 fusion.174
  644.8 1.4 fusion.173
  646.2 1.4 fusion.172
  650.2 0.6 constant_dynamic-slice_fusion.20
  656.4 1.4 fusion.174
  657.7 1.4 fusion.173
  659.1 1.4 fusion.172
  669.3 1.4 fusion.174
  670.7 1.4 fusion.173
  672.1 1.4 fusion.172
  676.1 0.6 constant_dynamic-slice_fusion.20
  682.3 1.4 fusion.174
  683.7 1.4 fusion.173
  685.1 1.4 fusion.172
  695.3 1.4 fusion.174
  696.7 1.4 fusion.173
  698.0 1.4 fusion.172
  (131 shorter events, 15.5 us)
Async XLA Ops:
  0.6 311.4 %copy-start = (f32[6,64,64]{2,1,0:T(8,128)S(1)}, f32[6,64,64]{2,1,0:T(8,128)}, u32[]{:S(2)}) copy-start(f32[6,64,64]{2,1,0:T(8,128)} %param.18) | copy-start | bytes 294916
  5.9 11.1 %copy-start.7 = (s32[1,32]{1,0:T(1,128)S(1)}, s32[1,32]{1,0:T(1,128)}, u32[]{:S(2)}) copy-start(s32[1,32]{1,0:T(1,128)} %param.14) | copy-start | bytes 388
  5.9 11.7 %copy-start.1 = (bf16[3072,512]{1,0:T(8,128)(2,1)S(1)}, bf16[3072,512]{1,0:T(8,128)(2,1)}, u32[]{:S(2)}) copy-start(bf16[3072,512]{1,0:T(8,128)(2,1)} %param.12) | copy-start | bytes 9437188
  5.9 193.3 %all-to-all-start = ((bf16[64,32,2048]{2,1,0:T(8,128)(2,1)}), bf16[64,32,2048]{2,1,0:T(8,128)(2,1)}, u32[]{:S(2)}, u32[]{:S(2)}) async-start(bf16[64,32,2048]{2,1,0:T(8,128)(2,1)} %stack.20), calls=%async_computation | async-start | bytes 16777216 | tf_op jit(solution)/shard_map/all_to_all | solution.py:80
  17.6 7.6 %copy-start.6 = (s32[3,6]{1,0:T(4,128)S(1)}, s32[3,6]{1,0:T(4,128)}, u32[]{:S(2)}) copy-start(s32[3,6]{1,0:T(4,128)} %param.15) | copy-start | bytes 220
  17.6 8.2 %copy-start.8 = (s32[1,8]{1,0:T(1,128)S(1)}, s32[1,8]{1,0:T(1,128)}, u32[]{:S(2)}) copy-start(s32[1,8]{1,0:T(1,128)} %param.21) | copy-start | bytes 100
  17.6 8.3 %copy-start.9 = (s32[1,64]{1,0:T(1,128)S(1)}, s32[1,64]{1,0:T(1,128)}, u32[]{:S(2)}) copy-start(s32[1,64]{1,0:T(1,128)} %param.20) | copy-start | bytes 772
  297.4 14.0 %copy-start.2 = (f32[64,3072]{1,0:T(8,128)S(1)}, f32[64,3072]{1,0:T(8,128)}, u32[]{:S(2)}) copy-start(f32[64,3072]{1,0:T(8,128)} %param.17) | copy-start | bytes 2359300
  297.4 15.0 %copy-start.3 = (f32[1,64,64]{2,1,0:T(8,128)S(1)}, f32[1,64,64]{2,1,0:T(8,128)}, u32[]{:S(2)}) copy-start(f32[1,64,64]{2,1,0:T(8,128)} %param.19) | copy-start | bytes 49156
  302.4 319.2 %copy-start.4 = (f32[3072]{0:T(1024)}, f32[3072]{0:T(1024)S(1)}, u32[]{:S(2)}) copy-start(f32[3072]{0:T(1024)S(1)} %fusion.63) | copy-start | bytes 36868
  302.4 319.2 %collective-permute-start = (f32[6,4,512]{2,1,0:T(4,128)S(1)}, f32[6,4,512]{2,1,0:T(4,128)S(1)}, u32[]{:S(2)}, u32[]{:S(2)}) collective-permute-start(f32[6,4,512]{2,1,0:T(4,128)S(1)} %pad_maximum_fusion.1), channel_id=1, source_target_pairs={{0,1},{1,2},{2,3},{3,4},{4,5},{5,6},{6,7},{7,8},{8,9},{9,10},{10,1... | collective-permute-start | bytes 147464 | tf_op jit(solution)/shard_map/ppermute | solution.py:23
  304.3 317.2 %collective-permute-start.1 = (f32[6,4,512]{2,1,0:T(4,128)S(1)}, f32[6,4,512]{2,1,0:T(4,128)S(1)}, u32[]{:S(2)}, u32[]{:S(2)}) collective-permute-start(f32[6,4,512]{2,1,0:T(4,128)S(1)} %pad_maximum_fusion.1), channel_id=1, source_target_pairs={{1,0},{2,1},{3,2},{4,3},{5,4},{6,5},{7,6},{8,7},{9,8},{10,9},{11,1... | collective-permute-start | bytes 147464 | tf_op jit(solution)/shard_map/ppermute | solution.py:24
  617.8 3.9 copy-start.5
